TPU v7x, 256 devices: a whole 4x4x8 slice. The times are simulated.
256 devices in a mesh: dp: 16 (over z, core), filter: 16 (over x, y).
Axes of the slice: x: 4, y: 4, z: 8, core: 2. Of those that a mesh axis runs over, the one named last changes fastest.
Arguments:
- patches: bfloat16 [256, 48, 2048], P('filter', 'dp'), may hold values from -6 to 6
- cotangent: bfloat16 [256, 48, 2048], P('filter', 'dp'), may hold values from -6 to 6
- first_weight: bfloat16 [27, 256, 256], P(None, 'filter'), may hold values from -0.078125 to 0.078125
- second_weight: bfloat16 [27, 256, 256], P(None, 'filter'), may hold values from -0.078125 to 0.078125
- counts: int32 [16], P('dp'), may hold values from 0 to 3, as said below
Outputs:
- output_maps: float32 [256, 48, 2048], P('filter', 'dp')
- input_grad: float32 [256, 48, 2048], P('filter', 'dp')
- first_grad: float32 [27, 256, 256], P(None, 'filter')
- second_grad: float32 [27, 256, 256], P(None, 'filter')
Inputs may be any that keep to these rules, and one draw needn't show every extreme that they name: The counts of all groups sum to 16; one group holds exactly 3 live patches. Live patches of a group occupy its first slots.
All inputs are finite; a program needn't handle non-finite values.
Results may differ from a plain program's by a relative error of at most 0.0029.
Values may be sent and summed in bfloat16 or wider, within the bound.
No kernel may reach another device: no remote copies, remote signals or barrier semaphores. Data moves between devices by JAX's collectives and lax.ppermute only.
A program may use at most 128 MiB of HBM per device.

v0:
```python
import jax
import jax.numpy as jnp
from jax import lax
from jax.sharding import PartitionSpec as P

PX = 8
PY = 16
PZ = 16
CAP = 3
CELLS = 2048
stencil_taps = [(ox, oy, oz) for ox in (-1, 0, 1) for oy in (-1, 0, 1) for oz in (-1, 0, 1)]


def shift_cells(value, ox, oy, oz):
    span = PY * PZ + PZ + 1
    step = ox * PY * PZ + oy * PZ + oz
    padded = jnp.pad(value, [(0, 0)] * (value.ndim - 1) + [(span, span)])
    moved = lax.slice_in_dim(padded, span + step, span + step + CELLS, axis=value.ndim - 1)
    cell = jnp.arange(CELLS, dtype=jnp.int32)
    pos_x = cell // (PY * PZ) + ox
    pos_y = cell // PZ % PY + oy
    pos_z = cell % PZ + oz
    inside = (pos_x >= 0) & (pos_x < PX) & (pos_y >= 0) & (pos_y < PY) & (pos_z >= 0) & (pos_z < PZ)
    return jnp.where(inside, moved, jnp.zeros_like(moved))


def shifted_stack(value):
    return jnp.stack([shift_cells(value, -ox, -oy, -oz) for ox, oy, oz in stencil_taps])


def forward_conv(inputs, weight):
    proj = jnp.einsum("toi,isc->tosc", weight, inputs, preferred_element_type=jnp.float32)
    total = jnp.zeros(proj.shape[1:], jnp.float32)
    for t, (ox, oy, oz) in enumerate(stencil_taps):
        total = total + shift_cells(proj[t], ox, oy, oz)
    return total


def weight_conv(grads, inputs):
    stack = shifted_stack(grads)
    return jnp.einsum("tosc,isc->toi", stack, inputs, preferred_element_type=jnp.float32)


def backward_conv(grads, weight):
    stack = shifted_stack(grads)
    return lax.psum_scatter(
        jnp.einsum("toi,tosc->isc", weight, stack, preferred_element_type=jnp.float32),
        "filter",
        scatter_dimension=0,
        tiled=True,
    )


def layer_pair(inputs, masked, first_weight, second_weight):
    full_inputs = lax.all_gather(inputs, "filter", axis=0, tiled=True)
    first = forward_conv(full_inputs, first_weight)
    hidden = jax.nn.silu(first).astype(jnp.bfloat16)
    full_hidden = lax.all_gather(hidden, "filter", axis=0, tiled=True)
    result = forward_conv(full_hidden, second_weight)
    hidden_grad = backward_conv(masked, second_weight)
    second_part = weight_conv(masked, full_hidden)
    sigma = jax.nn.sigmoid(first)
    delta = (hidden_grad * sigma * (1.0 + first * (1.0 - sigma))).astype(jnp.bfloat16)
    in_grad = backward_conv(delta, first_weight)
    first_part = weight_conv(delta, full_inputs)
    return (result, in_grad, first_part, second_part)


def shards(patches, cotangent, first_weight, second_weight, counts):
    live = (jnp.arange(CAP, dtype=jnp.int32) < counts[0]).astype(jnp.bfloat16)
    masked = cotangent * live[None, :, None]
    result, in_grad, first_part, second_part = layer_pair(
        patches, masked, first_weight, second_weight
    )
    output_maps = result * live[None, :, None].astype(jnp.float32)
    first_sum, second_sum = lax.psum((first_part, second_part), "dp")
    scale = 1.0 / jnp.sqrt(jnp.float32(lax.axis_size("dp") * CELLS))
    return (output_maps, in_grad, first_sum * scale, second_sum * scale)


def solution(mesh):
    placed = (
        P("filter", "dp", None),
        P("filter", "dp", None),
        P(None, "filter", None),
        P(None, "filter", None),
        P("dp"),
    )
    return jax.shard_map(
        shards,
        mesh=mesh,
        in_specs=placed,
        out_specs=(
            P("filter", "dp", None),
            P("filter", "dp", None),
            P(None, "filter", None),
            P(None, "filter", None),
        ),
        check_vma=False,
    )
```

profile of v0, /device:TPU:1, one launch (start us, length us, event | category | flops | bytes accessed | tf_op | source)
XLA Modules:
  0.0 506.1 jit_solution(9480231245878165293)
XLA Ops:
  7.2 0.7 all-gather.3.cloned.1.call-update
  8.9 1.0 broadcast_multiply_fusion.2
  11.0 0.1 fusion.153
  11.1 0.1 fusion.156
  11.2 0.1 fusion.159
  11.4 0.1 fusion.162
  11.6 0.1 fusion.165
  13.2 2.3 copy-done.2
  15.5 4.8 convolution_bitcast_fusion.2
  20.4 46.6 %all-gather.3.cloned.1.call-done = bf16[256,3,2048]{2,0,1:T(8,128)(2,1)} async-done(((bf16[16,3,2048]{2,0,1:T(8,128)(2,1)}), bf16[256,3,2048]{2,0,1:T(8,128)(2,1)}) %all-gather.3.cloned.1.call-update) | async-done | bytes 3145744 | tf_op jit(solution)/shard_map/all_gather | solution.py:55
  67.0 3.4 fusion.5
  70.5 0.2 slice_bitcast_fusion.52
  70.7 3.9 copy-done.4
  74.5 3.0 slice_bitcast_fusion.53
  77.5 77.9 %reduce-scatter.2.cloned.1.call-done = f32[16,3,2048]{2,0,1:T(8,128)} async-done(((f32[256,3,2048]{2,0,1:T(8,128)}), f32[16,3,2048]{2,0,1:T(8,128)}) %reduce-scatter.2.cloned.1.call-update) | async-done | bytes 393232 | tf_op jit(solution)/shard_map/reduce_scatter | solution.py:46
  155.4 4.9 multiply_convert_fusion
  160.3 0.8 fusion.204
  161.1 0.8 fusion.207
  161.9 0.8 fusion.210
  162.7 0.8 fusion.213
  163.5 0.7 fusion.216
  164.2 0.8 fusion.219
  165.0 0.8 fusion.222
  165.8 0.8 fusion.225
  166.6 0.8 fusion.228
  167.4 0.8 fusion.231
  168.2 0.8 fusion.234
  169.0 0.8 fusion.237
  169.8 0.8 fusion.240
  170.6 0.7 bitcast_dynamic-update-slice_fusion
  171.3 0.8 fusion.243
  172.1 0.8 fusion.246
  172.9 0.8 fusion.249
  173.7 0.8 fusion.252
  174.5 0.8 multiply_convert_fusion.1
  175.3 0.2 all-reduce.59.cloned.1.call-start
  175.6 0.8 fusion.255
  176.4 0.8 fusion.258
  177.2 0.8 fusion.261
  178.0 0.8 fusion.264
  178.8 0.7 fusion.267
  179.5 0.8 fusion.270
  180.3 0.8 fusion.273
  181.1 0.8 fusion.276
  181.8 0.8 fusion.279
  182.6 7.1 %convolution_bitcast_fusion.1 = f32[256,3,2048]{0,2,1:T(8,128)} fusion(bf16[27,16,3,2048]{3,1,2,0:T(8,128)(2,1)} %fusion.279, bf16[27,16,256]{2,1,0:T(8,128)(2,1)S(1)} %copy-done), kind=kOutput, calls=%fused_computation.1 | convolution fusion | flops 1358954496 | bytes 11821056 | tf_op jit(solution)/shard_map/toi,tosc->isc/dot_general | solution.py:47
  189.7 9.6 %copy.24 = f32[256,3,2048]{2,1,0:T(4,128)} copy(f32[256,3,2048]{0,2,1:T(8,128)} %convolution_bitcast_fusion.1) | data formatting | bytes 12582912 | tf_op jit(solution)/shard_map/toi,tosc->isc/dot_general | solution.py:47
  199.4 0.6 copy-done.8
  200.0 0.6 dynamic-slice
  201.2 5.8 %fusion.7 = f32[27,16,256]{2,1,0:T(8,128)} fusion(bf16[27,16,3,2048]{3,1,2,0:T(8,128)(2,1)} %fusion.279, bf16[256,3,2048]{2,0,1:T(8,128)(2,1)} %all-gather.3.cloned.1.call-done), kind=kOutput, calls=%fused_computation.10 | convolution fusion | flops 1358954496 | bytes 8896512 | tf_op jit(solution)/shard_map/tosc,isc->toi/dot_general | solution.py:41
  207.0 21.6 %all-gather.5.cloned.1.call-done = bf16[256,3,2048]{2,0,1:T(8,128)(2,1)} async-done(((bf16[16,3,2048]{2,0,1:T(8,128)(2,1)}), bf16[256,3,2048]{2,0,1:T(8,128)(2,1)}) %all-gather.5.cloned.1.call-update) | async-done | bytes 3145744 | tf_op jit(solution)/shard_map/all_gather | solution.py:58
  228.6 3.5 convolution_bitcast_fusion
  232.1 4.1 copy-done.3
  236.2 0.2 slice_bitcast_fusion.25
  236.4 1.7 copy-done.7
  238.1 4.8 fusion.10
  242.9 6.1 %slice_bitcast_fusion.26 = (f32[16,3,2048]{2,0,1:T(8,128)S(1)}, f32[16,3,2048]{2,0,1:T(8,128)}, f32[16,3,2048]{2,0,1:T(8,128)}, f32[16,3,2048]{2,0,1:T(8,128)}, ...) fusion(f32[27,16,3,2048]{3,1,2,0:T(8,128)} %copy-done.3), kind=kLoop, calls=%fused_computation.196 | loop fusion | bytes 14942208 | tf_op jit(solution)/shard_map/squeeze | solution.py:35
  249.0 6.4 %fusion.115 = f32[16,3,2048]{2,0,1:T(8,128)} fusion(f32[16,3,2048]{2,0,1:T(8,128)} %get-tuple-element.19, f32[16,3,2048]{2,0,1:T(8,128)} %get-tuple-element.18, f32[16,3,2048]{2,0,1:T(8,128)} %get-tuple-element.17, f32[16,3,2048]{2,0,1:T(8,128)} %get-tuple-element.20, f32[16,3,2048]{2,0,1:T(8,128)} %get-tuple-element.21, ...), kind=kLoop, calls=%fused_computation.166 | loop fusion | flops 5308416 | bytes 11065356 | tf_op jit(solution)/shard_map/mul | solution.py:75
  255.4 127.1 %all-reduce.59.cloned.1.call-done = f32[256,3,2048]{2,1,0:T(4,128)} async-done(((f32[256,3,2048]{2,1,0:T(4,128)}), f32[256,3,2048]{2,1,0:T(4,128)}) %all-reduce.59.cloned.1.call-update) | async-done | bytes 6291472
  382.5 1.1 constant_dynamic-slice_fusion
  383.6 1.0 copy.25
  384.6 111.3 %all-reduce.61.cloned.1.call-done = (f32[27,16,256]{2,1,0:T(8,128)}, f32[27,16,256]{2,1,0:T(8,128)}) async-done(((f32[27,16,256]{2,1,0:T(8,128)}, f32[27,16,256]{2,1,0:T(8,128)}), (f32[27,16,256]{2,1,0:T(8,128)}, f32[27,16,256]{2,1,0:T(8,128)})) %all-reduce.61.cloned.1.call-update) | async-done | bytes 884752 | tf_op jit(solution)/shard_map/psum | solution.py:76
  495.9 1.8 broadcast_multiply_fusion
  497.7 1.8 broadcast_multiply_fusion.1
  (59 shorter events, 2.9 us)
Async XLA Ops:
  7.2 59.8 %copy-start = (bf16[27,16,256]{2,1,0:T(8,128)(2,1)S(1)}, bf16[27,16,256]{2,1,0:T(8,128)(2,1)}, u32[]{:S(2)}) copy-start(bf16[27,16,256]{2,1,0:T(8,128)(2,1)} %param.7) | copy-start | bytes 663556
  7.2 4.3 copy-start.5
  7.2 59.8 %all-gather.3.cloned.1.call-start = ((), (), s32[]{:S(2)}) async-start(), calls=%async_computation.1 | async-start | bytes 3342336 | tf_op jit(solution)/shard_map/all_gather | solution.py:55
  7.9 147.5 %reduce-scatter.2.cloned.1.call-start = ((), (), s32[]{:S(2)}) async-start(), calls=%async_computation.3 | async-start | bytes 6684672 | tf_op jit(solution)/shard_map/reduce_scatter | solution.py:46
  9.9 5.6 %copy-start.6 = (bf16[27,16,256]{2,1,0:T(8,128)(2,1)S(1)}, bf16[27,16,256]{2,1,0:T(8,128)(2,1)}, u32[]{:S(2)}) copy-start(bf16[27,16,256]{2,1,0:T(8,128)(2,1)} %param.8) | copy-start | bytes 663556
  13.2 2.3 copy-start.2
  20.3 208.3 %all-gather.5.cloned.1.call-start = ((), (), s32[]{:S(2)}) async-start(), calls=%async_computation.2 | async-start | bytes 3342336 | tf_op jit(solution)/shard_map/all_gather | solution.py:58
  70.5 4.1 copy-start.4
  175.3 207.2 %all-reduce.59.cloned.1.call-start = ((), (), s32[]{:S(2)}) async-start(), calls=%async_computation.4 | async-start | bytes 16777216
  199.3 0.7 copy-start.8
  199.3 296.6 %all-reduce.61.cloned.1.call-start = ((), (), s32[]{:S(2)}) async-start(), calls=%async_computation.5 | async-start | bytes 1769472 | tf_op jit(solution)/shard_map/psum | solution.py:76
  232.1 4.1 copy-start.3
  236.2 1.9 copy-start.7
  249.0 250.6 %copy-start.1 = (bf16[27,16,256]{2,1,0:T(8,128)(2,1)S(1)}, bf16[27,16,256]{2,1,0:T(8,128)(2,1)}, u32[]{:S(2)}) copy-start(bf16[27,16,256]{2,1,0:T(8,128)(2,1)} %param.7) | copy-start | bytes 663556
Sparse Core Ops, SparseCore 0:
  10.5 56.4 all-gather.2
  70.7 84.6 reduce-scatter.1
  175.4 53.1 all-gather.4
  232.0 150.3 all-reduce.58
  385.5 110.4 all-reduce.60
where the time goes:
time: 507 us; the launch traced here: 506 us
  waiting for transfers between devices  385 us (76%)
  other arithmetic  41.3 us (8%)
  local copies, waits for them, and re-layouts  34.3 us (7%)
  matrix products  29.5 us (6%)
  between operations  15.5 us (3%)
    unnamed x6, waiting for transfers between devices  128 us
    psum x1, waiting for transfers between devices, shards(): first_sum, second_sum = lax.psum((first_part, second_part), 'dp')  111 us
    reduce_scatter x1, waiting for transfers between devices, backward_conv(): lax.psum_scatter(jnp.einsum('toi,tosc->isc', weight, stack, preferred_ele...  77.9 us
    all_gather x1, waiting for transfers between devices, layer_pair(): full_inputs = lax.all_gather(inputs, 'filter', axis=0, tiled=True)  46.6 us
    unnamed x52, other arithmetic  23.4 us
    all_gather x1, waiting for transfers between devices, layer_pair(): full_hidden = lax.all_gather(hidden, 'filter', axis=0, tiled=True)  21.6 us
    unnamed x21, local copies, waits for them, and re-layouts  15.2 us
    dot_general x2, matrix products, backward_conv(): jnp.einsum('toi,tosc->isc', weight, stack, preferred_element_type=jnp.flo...  11.9 us
  transfers between devices with their start and end apart: 5, of which 5 were waited for; matrix products, arithmetic and copies ran while one was open for 14% of the time, Pallas kernels for 0%

commit v1 on v0

--- a/solution.py
+++ b/solution.py
@@ -55,7 +55,9 @@
     full_inputs = lax.all_gather(inputs, "filter", axis=0, tiled=True)
     first = forward_conv(full_inputs, first_weight)
     hidden = jax.nn.silu(first).astype(jnp.bfloat16)
-    full_hidden = lax.all_gather(hidden, "filter", axis=0, tiled=True)
+    full_hidden = jnp.concatenate(
+        lax.all_to_all(jnp.stack([hidden] * lax.axis_size("filter")), "filter", 0, 0), axis=0
+    )
     result = forward_conv(full_hidden, second_weight)
     hidden_grad = backward_conv(masked, second_weight)
     second_part = weight_conv(masked, full_hidden)

time: 507 us -> 497 us (0.980)
  other arithmetic: 41.3 us -> 23.3 us
  waiting for transfers between devices: 385 us -> 393 us
    all_to_all x0 -> x1, waiting for transfers between devices: none -> 26.1 us  [layer_pair(): lax.all_to_all(jnp.stack([hidden] * lax.axis_size('filter')), 'filter', 0...]
    unnamed x6 -> x5, waiting for transfers between devices: 128 us -> 153 us
    all_gather x1 -> x0, waiting for transfers between devices: 21.6 us -> none  [layer_pair(): full_hidden = lax.all_gather(hidden, 'filter', axis=0, tiled=True)]
    psum x1, waiting for transfers between devices: 111 us -> 90.1 us  [shards(): first_sum, second_sum = lax.psum((first_part, second_part), 'dp')]
    unnamed x52, other arithmetic: 23.4 us -> 9.26 us
    unnamed x21 -> x17, local copies, waits for them, and re-layouts: 15.2 us -> 11.9 us
  transfers between devices with their start and end apart: 5 -> 5, of which waited for: 5 -> 5; matrix products, arithmetic and copies ran while one was open for 14% -> 11% of each run, Pallas kernels for 0% -> 0%
where the time goes in v1:
time: 497 us; the launch traced here: 496 us
  waiting for transfers between devices  393 us (79%)
  local copies, waits for them, and re-layouts  30.1 us (6%)
  matrix products  28.6 us (6%)
  other arithmetic  23.3 us (5%)
  between operations  15.6 us (3%)
  starting transfers between devices  4.98 us (1%)
    unnamed x5, waiting for transfers between devices  153 us
    psum x1, waiting for transfers between devices, shards(): first_sum, second_sum = lax.psum((first_part, second_part), 'dp')  90.1 us
    reduce_scatter x1, waiting for transfers between devices, backward_conv(): lax.psum_scatter(jnp.einsum('toi,tosc->isc', weight, stack, preferred_ele...  77.9 us
    all_gather x1, waiting for transfers between devices, layer_pair(): full_inputs = lax.all_gather(inputs, 'filter', axis=0, tiled=True)  46.6 us
    all_to_all x1, waiting for transfers between devices, layer_pair(): lax.all_to_all(jnp.stack([hidden] * lax.axis_size('filter')), 'filter', 0...  26.1 us
    dot_general x2, matrix products, backward_conv(): jnp.einsum('toi,tosc->isc', weight, stack, preferred_element_type=jnp.flo...  11.9 us
    unnamed x17, local copies, waits for them, and re-layouts  11.9 us
    dot_general x2, matrix products, weight_conv(): jnp.einsum('tosc,isc->toi', stack, inputs, preferred_element_type=jnp.flo...  10.7 us
  transfers between devices with their start and end apart: 5, of which 5 were waited for; matrix products, arithmetic and copies ran while one was open for 11% of the time, Pallas kernels for 0%

profile of v1, /device:TPU:1, one launch (start us, length us, event | category | flops | bytes accessed | tf_op | source)
XLA Modules:
  0.0 495.8 jit_solution(17488840797564924927)
XLA Ops:
  7.2 0.7 all-gather.2.cloned.1.call-update
  8.9 1.0 broadcast_multiply_fusion.2
  10.5 0.1 fusion.135
  10.6 0.1 fusion.138
  10.7 0.1 fusion.141
  10.8 0.1 fusion.144
  11.0 0.1 fusion.147
  11.1 0.1 fusion.150
  11.2 0.1 fusion.153
  11.4 0.1 fusion.156
  11.5 0.1 bitcast_dynamic-update-slice_fusion.1
  11.6 0.1 fusion.159
  11.7 0.1 fusion.162
  11.9 0.1 fusion.165
  12.0 0.1 fusion.168
  12.1 0.1 fusion.171
  12.3 0.1 fusion.174
  12.4 0.1 fusion.177
  13.2 2.3 copy-done.1
  15.5 4.8 convolution_bitcast_fusion.2
  20.4 46.6 %all-gather.2.cloned.1.call-done = bf16[256,3,2048]{2,0,1:T(8,128)(2,1)} async-done(((bf16[16,3,2048]{2,0,1:T(8,128)(2,1)}), bf16[256,3,2048]{2,0,1:T(8,128)(2,1)}) %all-gather.2.cloned.1.call-update) | async-done | bytes 3145744 | tf_op jit(solution)/shard_map/all_gather | solution.py:55
  67.0 3.4 fusion.2
  70.5 0.2 slice_bitcast_fusion.52
  70.7 3.9 copy-done.2
  74.5 3.0 slice_bitcast_fusion.53
  77.5 77.9 %reduce-scatter.2.cloned.1.call-done = f32[16,3,2048]{2,0,1:T(8,128)} async-done(((f32[256,3,2048]{2,0,1:T(8,128)}), f32[16,3,2048]{2,0,1:T(8,128)}) %reduce-scatter.2.cloned.1.call-update) | async-done | bytes 393232 | tf_op jit(solution)/shard_map/reduce_scatter | solution.py:46
  155.4 4.9 multiply_convert_fusion
  161.1 0.1 fusion.219
  161.4 0.1 fusion.225
  161.5 0.1 fusion.228
  161.6 0.1 fusion.231
  161.8 0.1 fusion.234
  161.9 0.1 fusion.237
  162.1 0.1 fusion.240
  162.2 0.1 fusion.243
  162.3 0.1 fusion.246
  162.9 2.3 copy-done.5
  165.3 2.0 stack.114
  167.3 4.6 all-to-all-start
  172.0 0.2 all-reduce.61.cloned.1.call-start
  172.2 0.8 fusion.258
  173.1 0.7 fusion.261
  173.8 0.8 fusion.264
  174.6 0.8 fusion.267
  175.4 0.8 fusion.270
  176.2 0.8 fusion.273
  177.0 5.8 %fusion.4 = f32[27,16,256]{2,1,0:T(8,128)} fusion(bf16[27,16,3,2048]{3,1,2,0:T(8,128)(2,1)} %fusion.273, bf16[256,3,2048]{2,0,1:T(8,128)(2,1)} %all-gather.2.cloned.1.call-done), kind=kOutput, calls=%fused_computation.7 | convolution fusion | flops 1358954496 | bytes 8896512 | tf_op jit(solution)/shard_map/tosc,isc->toi/dot_general | solution.py:41
  182.8 26.1 %all-to-all-done = bf16[16,16,3,2048]{3,1,2,0:T(8,128)(2,1)} async-done(((bf16[16,16,3,2048]{3,1,2,0:T(8,128)(2,1)}), bf16[16,16,3,2048]{3,1,2,0:T(8,128)(2,1)}, u32[]{:S(2)}, u32[]{:S(2)}) %all-to-all-start) | async-done | bytes 3145760 | tf_op jit(solution)/shard_map/all_to_all | solution.py:59
  208.9 2.1 copy.17
  211.0 4.8 convolution_bitcast_fusion.3
  215.9 7.1 %convolution_bitcast_fusion.1 = f32[256,3,2048]{0,2,1:T(8,128)} fusion(bf16[27,16,3,2048]{3,1,2,0:T(8,128)(2,1)} %fusion.273, bf16[27,16,256]{2,1,0:T(8,128)(2,1)S(1)} %copy-done), kind=kOutput, calls=%fused_computation.1 | convolution fusion | flops 1358954496 | bytes 11821056 | tf_op jit(solution)/shard_map/toi,tosc->isc/dot_general | solution.py:47
  223.0 9.7 %copy.25 = f32[256,3,2048]{2,1,0:T(4,128)} copy(f32[256,3,2048]{0,2,1:T(8,128)} %convolution_bitcast_fusion.1) | data formatting | bytes 12582912 | tf_op jit(solution)/shard_map/toi,tosc->isc/dot_general | solution.py:47
  232.7 0.6 copy-done.6
  233.4 0.6 dynamic-slice
  234.6 2.6 convolution_bitcast_fusion
  237.2 0.3 slice_bitcast_fusion.25
  237.5 1.0 slice_bitcast_fusion.26
  238.4 3.2 fusion.109
  241.7 90.1 %all-reduce.61.cloned.1.call-done = (f32[27,16,256]{2,1,0:T(8,128)}, f32[27,16,256]{2,1,0:T(8,128)}) async-done(((f32[27,16,256]{2,1,0:T(8,128)}, f32[27,16,256]{2,1,0:T(8,128)}), (f32[27,16,256]{2,1,0:T(8,128)}, f32[27,16,256]{2,1,0:T(8,128)})) %all-reduce.61.cloned.1.call-update) | async-done | bytes 884752 | tf_op jit(solution)/shard_map/psum | solution.py:78
  331.7 1.8 broadcast_multiply_fusion
  333.6 1.8 broadcast_multiply_fusion.1
  335.4 151.8 %all-reduce.59.cloned.1.call-done = f32[256,3,2048]{2,1,0:T(4,128)} async-done(((f32[256,3,2048]{2,1,0:T(4,128)}), f32[256,3,2048]{2,1,0:T(4,128)}) %all-reduce.59.cloned.1.call-update) | async-done | bytes 6291472
  487.2 1.1 constant_dynamic-slice_fusion
  488.3 1.0 copy.26
  (56 shorter events, 2.9 us)
Async XLA Ops:
  7.2 59.8 %copy-start = (bf16[27,16,256]{2,1,0:T(8,128)(2,1)S(1)}, bf16[27,16,256]{2,1,0:T(8,128)(2,1)}, u32[]{:S(2)}) copy-start(bf16[27,16,256]{2,1,0:T(8,128)(2,1)} %param.7) | copy-start | bytes 663556
  7.2 4.3 copy-start.3
  7.2 59.8 %all-gather.2.cloned.1.call-start = ((), (), s32[]{:S(2)}) async-start(), calls=%async_computation.2 | async-start | bytes 3342336 | tf_op jit(solution)/shard_map/all_gather | solution.py:55
  7.9 147.5 %reduce-scatter.2.cloned.1.call-start = ((), (), s32[]{:S(2)}) async-start(), calls=%async_computation.3 | async-start | bytes 6684672 | tf_op jit(solution)/shard_map/reduce_scatter | solution.py:46
  9.9 5.6 %copy-start.4 = (bf16[27,16,256]{2,1,0:T(8,128)(2,1)S(1)}, bf16[27,16,256]{2,1,0:T(8,128)(2,1)}, u32[]{:S(2)}) copy-start(bf16[27,16,256]{2,1,0:T(8,128)(2,1)} %param.8) | copy-start | bytes 663556
  13.2 2.3 copy-start.1
  70.5 4.1 copy-start.2
  162.8 2.4 copy-start.5
  167.3 41.5 %all-to-all-start = ((bf16[16,16,3,2048]{3,1,2,0:T(8,128)(2,1)}), bf16[16,16,3,2048]{3,1,2,0:T(8,128)(2,1)}, u32[]{:S(2)}, u32[]{:S(2)}) async-start(bf16[16,16,3,2048]{3,1,2,0:T(8,128)(2,1)} %stack.114), calls=%async_computation | async-start | bytes 6291456 | tf_op jit(solution)/shard_map/all_to_all | solution.py:59
  172.0 159.7 %all-reduce.61.cloned.1.call-start = ((), (), s32[]{:S(2)}) async-start(), calls=%async_computation.5 | async-start | bytes 1769472 | tf_op jit(solution)/shard_map/psum | solution.py:78
  215.9 271.3 %all-reduce.59.cloned.1.call-start = ((), (), s32[]{:S(2)}) async-start(), calls=%async_computation.4 | async-start | bytes 16777216
  232.7 0.7 copy-start.6
Sparse Core Ops, SparseCore 0:
  10.5 56.4 all-gather.1
  70.7 84.6 reduce-scatter.1
  216.0 115.7 all-reduce.60
  335.6 151.5 all-reduce.58
